TPU v7x, 512 devices: a whole 4x4x16 slice. The times are simulated.
512 devices in a mesh: dp: 32 (over z_lo, x), tensor: 16 (over z_hi, y, core).
Axes of the slice: x: 4, y: 4, z: 16 (z_hi: 2, z_lo: 8; z = z_hi * 8 + z_lo), core: 2. Of those that a mesh axis runs over, the one named last changes fastest.
Arguments:
- out_grad: bfloat16 [4096, 4096], P(('dp', 'tensor')), may hold values from -6 to 6
- gate_pre: bfloat16 [4096, 14336], P('dp', 'tensor'), may hold values from -6 to 6
- up_pre: bfloat16 [4096, 14336], P('dp', 'tensor'), may hold values from -6 to 6
- down_weight: bfloat16 [14336, 4096], P('tensor', 'dp'), may hold values from -6 to 6
- moment: float32 [14336, 4096], P('tensor', 'dp'), may hold values from -4 to 4
- second: float32 [14336, 4096], P('tensor', 'dp'), may hold values from 0.01 to 0.5
- decay_mask: int32 [14336], P('tensor'), may hold values 0 or 1
Outputs:
- grad_gate: bfloat16 [4096, 14336], P('dp', 'tensor')
- grad_up: bfloat16 [4096, 14336], P('dp', 'tensor')
- new_weight: bfloat16 [14336, 4096], P('tensor', 'dp')
- new_moment: float32 [14336, 4096], P('tensor', 'dp')
- new_second: float32 [14336, 4096], P('tensor', 'dp')
All inputs are finite; a program needn't handle non-finite values. No bound on the sum of `decay_mask` on one device may be relied on, other than what follows from the above.
Results may differ from a plain program's by a relative error of at most 0.0014.
Values may be sent and summed in bfloat16 or wider, within the bound.
A program may use at most 64 MiB of HBM per device.

v0:
```python
import math

import jax
import jax.numpy as jnp
from jax import lax
from jax.sharding import PartitionSpec as P

FF = 14336
OPT_STEP = 10


BETA_ONE = 0.9
BETA_TWO = 0.95
LEARN_RATE = 0.1
DECAY_RATE = 0.5
ADAM_EPS = 1e-08


def body(out_grad, gate_pre, up_pre, down_weight, moment, second, decay_mask):
    factor = 1.0 / math.sqrt(FF)
    group_grad = lax.all_gather(out_grad, "tensor", axis=0, tiled=True)
    gate = gate_pre.astype(jnp.float32)
    up = up_pre.astype(jnp.float32)
    sigmoid_gate = jax.nn.sigmoid(gate)
    activated = gate * sigmoid_gate
    hidden = (activated * up).astype(jnp.bfloat16)
    columns = lax.all_to_all(group_grad, "dp", split_axis=1, concat_axis=0, tiled=True)
    back_sum = lax.dot_general(
        group_grad,
        lax.all_gather(down_weight, "dp", axis=1, tiled=True),
        (((1,), (1,)), ((), ())),
        preferred_element_type=jnp.float32,
    )
    grad_sum = lax.dot_general(
        lax.all_gather(hidden, "dp", axis=0, tiled=True),
        columns,
        (((0,), (0,)), ((), ())),
        preferred_element_type=jnp.float32,
    )
    back = back_sum * factor
    grad_up = (back * activated).astype(jnp.bfloat16)
    grad_gate = (back * up * sigmoid_gate * (1.0 + gate * (1.0 - sigmoid_gate))).astype(
        jnp.bfloat16
    )
    weight_grad = grad_sum * factor
    new_moment = BETA_ONE * moment + (1.0 - BETA_ONE) * weight_grad
    new_second = BETA_TWO * second + (1.0 - BETA_TWO) * weight_grad * weight_grad
    fix_one = 1.0 - BETA_ONE**OPT_STEP
    fix_two = 1.0 - BETA_TWO**OPT_STEP
    weight = down_weight.astype(jnp.float32)
    decay = decay_mask.astype(jnp.float32)[:, None]
    direction = (
        new_moment / fix_one / (jnp.sqrt(new_second / fix_two) + ADAM_EPS)
        + DECAY_RATE * decay * weight
    )
    new_weight = (weight - LEARN_RATE * direction).astype(jnp.bfloat16)
    return (grad_gate, grad_up, new_weight, new_moment, new_second)


def solution(mesh):
    return jax.shard_map(
        body,
        mesh=mesh,
        in_specs=(
            P(("dp", "tensor"), None),
            P("dp", "tensor"),
            P("dp", "tensor"),
            P("tensor", "dp"),
            P("tensor", "dp"),
            P("tensor", "dp"),
            P("tensor"),
        ),
        out_specs=(
            P("dp", "tensor"),
            P("dp", "tensor"),
            P("tensor", "dp"),
            P("tensor", "dp"),
            P("tensor", "dp"),
        ),
        check_vma=False,
    )
```

profile of v0, /device:TPU:16, one launch (start us, length us, event | category | flops | bytes accessed | tf_op | source)
XLA Modules:
  0.0 545.6 jit_solution(17332230179337049735)
XLA Ops:
  7.2 0.0 all-gather.4.cloned.1.call-start
  7.2 0.7 all-gather.4.cloned.1.call-update
  7.9 0.0 all-gather.6.cloned.1.call-start
  7.9 0.7 all-gather.6.cloned.1.call-update
  8.7 0.0 copy-start.2
  8.7 0.0 copy-start.1
  8.7 0.0 copy-start.3
  8.7 0.0 copy-start.4
  8.7 0.0 all-gather.8.cloned.1.call-start
  8.7 83.2 %all-gather.4.cloned.1.call-done = bf16[128,4096]{1,0:T(8,128)(2,1)} async-done(((bf16[8,4096]{1,0:T(8,128)(2,1)}), bf16[128,4096]{1,0:T(8,128)(2,1)}) %all-gather.4.cloned.1.call-update) | async-done | bytes 1048592 | tf_op jit(solution)/shard_map/all_gather | solution.py:21
  91.9 200.6 %all-gather.6.cloned.1.call-done = bf16[896,4096]{1,0:T(8,128)(2,1)} async-done(((bf16[896,128]{1,0:T(8,128)(2,1)}), bf16[896,4096]{1,0:T(8,128)(2,1)}) %all-gather.6.cloned.1.call-update) | async-done | bytes 7340048 | tf_op jit(solution)/shard_map/all_gather | solution.py:30
  292.5 6.7 %multiply_convert_fusion = (bf16[128,896]{1,0:T(8,128)(2,1)}, bf16[128,896]{1,0:T(8,128)(2,1)}, bf16[128,896]{1,0:T(8,128)(2,1)}) fusion(bf16[128,896]{1,0:T(8,128)(2,1)} %param.8, bf16[128,896]{1,0:T(8,128)(2,1)} %param.9, bf16[128,4096]{1,0:T(8,128)(2,1)} %all-gather.4.cloned.1.call-done, bf16[896,4096]{1,0:T(8,128)(2,1)} %all-gather.6.cloned.1.call-done), kind=kOutput, calls=%fused_computation.21 | convolution fusion | flops 941588480 | bytes 9535488 | tf_op jit(solution)/shard_map/dot_general | solution.py:28
  299.2 0.0 all-gather.8.cloned.1.call-update
  299.2 0.0 copy-done
  299.2 1.4 copy.14
  300.6 9.5 %all-to-all-start = ((bf16[128,32,128]{0,2,1:T(8,128)(2,1)}), bf16[128,32,128]{0,2,1:T(8,128)(2,1)S(1)}, u32[]{:S(2)}, u32[]{:S(2)}) async-start(bf16[128,32,128]{0,2,1:T(8,128)(2,1)} %bitcast), calls=%async_computation | async-start | bytes 2097152 | tf_op jit(solution)/shard_map/all_to_all | solution.py:27
  310.1 0.0 copy-done.2
  310.1 51.3 %all-to-all-done = bf16[128,32,128]{0,2,1:T(8,128)(2,1)S(1)} async-done(((bf16[128,32,128]{0,2,1:T(8,128)(2,1)}), bf16[128,32,128]{0,2,1:T(8,128)(2,1)S(1)}, u32[]{:S(2)}, u32[]{:S(2)}) %all-to-all-start) | async-done | bytes 1048608 | tf_op jit(solution)/shard_map/all_to_all | solution.py:27
  361.4 0.7 copy.15
  362.1 170.6 %all-gather.8.cloned.1.call-done = bf16[4096,896]{1,0:T(8,128)(2,1)} async-done(((bf16[128,896]{1,0:T(8,128)(2,1)}), bf16[4096,896]{1,0:T(8,128)(2,1)}) %all-gather.8.cloned.1.call-update) | async-done | bytes 7340048 | tf_op jit(solution)/shard_map/all_gather | solution.py:35
  532.6 0.0 copy-done.1
  532.6 0.0 copy-done.3
  532.6 0.0 copy-done.4
  532.7 6.4 %fusion.6 = (bf16[896,128]{1,0:T(8,128)(2,1)}, f32[896,128]{1,0:T(8,128)}, f32[896,128]{1,0:T(8,128)}) fusion(bf16[896,128]{1,0:T(8,128)(2,1)S(1)} %copy-done.1, f32[896]{0:T(1024)S(1)} %convert_multiply_fusion.5, f32[896,128]{1,0:T(8,128)S(1)} %copy-done.3, f32[896,128]{1,0:T(8,128)S(1)} %copy-done.4, bf16[4096,896]{1,0:T(8,128)(2,1)} %all-gather.8.cloned.1.call-done, ...), kind=kOutput, calls=%fused_computation.14 | convolution fusion | flops 941588480 | bytes 10685952 | tf_op jit(solution)/shard_map/dot_general | solution.py:34
  (2 shorter events, 0.0 us)
Async XLA Ops:
  7.2 84.7 %all-gather.4.cloned.1.call-start = ((), (), s32[]{:S(2)}) async-start(), calls=%async_computation.1 | async-start | bytes 1114112 | tf_op jit(solution)/shard_map/all_gather | solution.py:21
  7.9 284.6 %all-gather.6.cloned.1.call-start = ((), (), s32[]{:S(2)}) async-start(), calls=%async_computation.2 | async-start | bytes 7569408 | tf_op jit(solution)/shard_map/all_gather | solution.py:30
  8.7 301.5 %copy-start.2 = (s32[896]{0:T(1024)S(1)}, s32[896]{0:T(1024)}, u32[]{:S(2)}) copy-start(s32[896]{0:T(1024)} %param.13) | copy-start | bytes 10756
  8.7 524.0 %copy-start.1 = (bf16[896,128]{1,0:T(8,128)(2,1)S(1)}, bf16[896,128]{1,0:T(8,128)(2,1)}, u32[]{:S(2)}) copy-start(bf16[896,128]{1,0:T(8,128)(2,1)} %param.10) | copy-start | bytes 688132
  8.7 524.0 %copy-start.3 = (f32[896,128]{1,0:T(8,128)S(1)}, f32[896,128]{1,0:T(8,128)}, u32[]{:S(2)}) copy-start(f32[896,128]{1,0:T(8,128)} %param.11) | copy-start | bytes 1376260
  8.7 524.0 %copy-start.4 = (f32[896,128]{1,0:T(8,128)S(1)}, f32[896,128]{1,0:T(8,128)}, u32[]{:S(2)}) copy-start(f32[896,128]{1,0:T(8,128)} %param.12) | copy-start | bytes 1376260
  8.7 524.0 %all-gather.8.cloned.1.call-start = ((), (), s32[]{:S(2)}) async-start(), calls=%async_computation.3 | async-start | bytes 7569408 | tf_op jit(solution)/shard_map/all_gather | solution.py:35
  91.9 207.3 %copy-start = (bf16[128,4096]{1,0:T(8,128)(2,1)S(1)}, bf16[128,4096]{1,0:T(8,128)(2,1)}, u32[]{:S(2)}) copy-start(bf16[128,4096]{1,0:T(8,128)(2,1)} %all-gather.4.cloned.1.call-done) | copy-start | bytes 3145732
  300.6 60.8 %all-to-all-start = ((bf16[128,32,128]{0,2,1:T(8,128)(2,1)}), bf16[128,32,128]{0,2,1:T(8,128)(2,1)S(1)}, u32[]{:S(2)}, u32[]{:S(2)}) async-start(bf16[128,32,128]{0,2,1:T(8,128)(2,1)} %bitcast), calls=%async_computation | async-start | bytes 2097152 | tf_op jit(solution)/shard_map/all_to_all | solution.py:27
Sparse Core Ops, SparseCore 0:
  11.3 80.5 all-gather.3
  93.9 198.5 all-gather.5
  299.3 233.2 all-gather.7
where the time goes:
time: 546 us
  waiting for transfers between devices  507 us (93%)
  between operations  13.8 us (3%)
  matrix products  13.2 us (2%)
  starting transfers between devices  9.62 us (2%)
    all_gather x1, waiting for transfers between devices, body(): lax.all_gather(down_weight, 'dp', axis=1, tiled=True)  201 us
    all_gather x1, waiting for transfers between devices, body(): lax.all_gather(hidden, 'dp', axis=0, tiled=True)  171 us
    all_gather x1, waiting for transfers between devices, body(): group_grad = lax.all_gather(out_grad, 'tensor', axis=0, tiled=True)  83.2 us
    all_to_all x1, waiting for transfers between devices, body(): lax.all_to_all(group_grad, 'dp', split_axis=1, concat_axis=0, tiled=True)  51.3 us
  transfers between devices with their start and end apart: 4, of which 4 were waited for; matrix products, arithmetic and copies ran while one was open for 0% of the time, Pallas kernels for 0%

commit v1 on v0

v1 whole, which is shorter than its diff:
```python
import math

import jax
import jax.numpy as jnp
from jax import lax
from jax.sharding import Mesh
from jax.sharding import PartitionSpec as P

FF = 14336
OPT_STEP = 10


BETA_ONE = 0.9
BETA_TWO = 0.95
LEARN_RATE = 0.1
DECAY_RATE = 0.5
ADAM_EPS = 1e-08

DP = ("zl", "x")
TP = ("zh", "y", "c")


def body(out_grad, gate_pre, up_pre, down_weight, moment, second, decay_mask):
    factor = 1.0 / math.sqrt(FF)
    group_grad = lax.all_gather(out_grad, "c", axis=0, tiled=True)
    group_grad = lax.all_gather(group_grad, "y", axis=0, tiled=True)
    group_grad = lax.all_gather(group_grad, "zh", axis=0, tiled=True)
    gate = gate_pre.astype(jnp.float32)
    up = up_pre.astype(jnp.float32)
    sigmoid_gate = jax.nn.sigmoid(gate)
    activated = gate * sigmoid_gate
    hidden = (activated * up).astype(jnp.bfloat16)
    columns = lax.all_to_all(group_grad, DP, split_axis=1, concat_axis=0, tiled=True)
    stacked = jnp.stack([down_weight, hidden.T])
    stacked = lax.all_gather(stacked, "x", axis=2, tiled=True)
    stacked = lax.all_gather(stacked, "zl", axis=2, tiled=True)
    back_sum = lax.dot_general(
        group_grad,
        stacked[0],
        (((1,), (1,)), ((), ())),
        preferred_element_type=jnp.float32,
    )
    grad_sum = lax.dot_general(
        stacked[1],
        columns,
        (((1,), (0,)), ((), ())),
        preferred_element_type=jnp.float32,
    )
    back = back_sum * factor
    grad_up = (back * activated).astype(jnp.bfloat16)
    grad_gate = (back * up * sigmoid_gate * (1.0 + gate * (1.0 - sigmoid_gate))).astype(
        jnp.bfloat16
    )
    weight_grad = grad_sum * factor
    new_moment = BETA_ONE * moment + (1.0 - BETA_ONE) * weight_grad
    new_second = BETA_TWO * second + (1.0 - BETA_TWO) * weight_grad * weight_grad
    fix_one = 1.0 - BETA_ONE**OPT_STEP
    fix_two = 1.0 - BETA_TWO**OPT_STEP
    weight = down_weight.astype(jnp.float32)
    decay = decay_mask.astype(jnp.float32)[:, None]
    direction = (
        new_moment / fix_one / (jnp.sqrt(new_second / fix_two) + ADAM_EPS)
        + DECAY_RATE * decay * weight
    )
    new_weight = (weight - LEARN_RATE * direction).astype(jnp.bfloat16)
    return (grad_gate, grad_up, new_weight, new_moment, new_second)


def solution(mesh):
    zl, x = 8, mesh.shape["dp"] // 8
    zh = mesh.shape["tensor"] // 8
    fine = Mesh(mesh.devices.reshape(zl, x, zh, 4, 2), DP + TP)
    return jax.shard_map(
        body,
        mesh=fine,
        in_specs=(
            P(DP + TP, None),
            P(DP, TP),
            P(DP, TP),
            P(TP, DP),
            P(TP, DP),
            P(TP, DP),
            P(TP),
        ),
        out_specs=(
            P(DP, TP),
            P(DP, TP),
            P(TP, DP),
            P(TP, DP),
            P(TP, DP),
        ),
        check_vma=False,
    )
```

time: 546 us -> 485 us (0.89)
  the two profiles are of different devices: /device:TPU:16 before, /device:TPU:105 now
where the time goes in v1:
time: 485 us
  waiting for transfers between devices  429 us (88%)
  between operations  13.8 us (3%)
  blocking collectives  13.3 us (3%)
  matrix products  11.8 us (2%)
  starting transfers between devices  7.26 us (1%)
  local copies, waits for them, and re-layouts  6.87 us (1%)
    all_gather x1, waiting for transfers between devices, body(): stacked = lax.all_gather(stacked, 'zl', axis=2, tiled=True)  231 us
    all_to_all x1, waiting for transfers between devices, body(): lax.all_to_all(group_grad, DP, split_axis=1, concat_axis=0, tiled=True)  92 us
    all_gather x1, waiting for transfers between devices, body(): group_grad = lax.all_gather(group_grad, 'zh', axis=0, tiled=True)  76.9 us
    all_gather x1, waiting for transfers between devices, body(): stacked = lax.all_gather(stacked, 'x', axis=2, tiled=True)  29.2 us
    all_gather x1, blocking collectives, body(): group_grad = lax.all_gather(group_grad, 'y', axis=0, tiled=True)  10.8 us
  transfers between devices with their start and end apart: 4, of which 4 were waited for; matrix products, arithmetic and copies ran while one was open for 1% of the time, Pallas kernels for 0%

profile of v1, /device:TPU:105, one launch (start us, length us, event | category | flops | bytes accessed | tf_op | source)
XLA Modules:
  0.0 484.9 jit_solution(10351806163342086163)
XLA Ops:
  7.2 0.0 all-gather.4.cloned.1.call-start
  7.2 1.1 copy.26
  8.3 1.1 copy.27
  9.4 0.1 fusion.15
  9.6 1.8 pad_maximum_fusion
  11.4 0.0 all-gather.4.cloned.1.call-update
  11.4 0.0 all-gather.8.cloned.1.call-start
  11.5 2.4 all_gather.17
  13.9 10.8 %all_gather.18 = bf16[64,4096]{1,0:T(8,128)(2,1)} all-gather(bf16[16,4096]{1,0:T(8,128)(2,1)S(1)} %all_gather.17), channel_id=1, replica_groups=mesh['zl'=8,'x'=4,'zh'=2,'y'=4,'c'=2] {'y'}, dimensions={0}, use_global_device_ids=true | all-gather | bytes 655360 | tf_op jit(solution)/shard_map/all_gather | solution.py:26
  24.8 0.0 all-gather.8.cloned.1.call-update
  24.8 0.0 all-gather.6.cloned.1.call-start
  24.9 29.2 %all-gather.4.cloned.1.call-done = bf16[2,896,512]{2,1,0:T(8,128)(2,1)} async-done(((bf16[2,896,128]{2,1,0:T(8,128)(2,1)}), bf16[2,896,512]{2,1,0:T(8,128)(2,1)}) %all-gather.4.cloned.1.call-update) | async-done | bytes 1835024 | tf_op jit(solution)/shard_map/all_gather | solution.py:35
  54.0 0.0 all-gather.6.cloned.1.call-update
  54.0 76.9 %all-gather.8.cloned.1.call-done = bf16[128,4096]{1,0:T(8,128)(2,1)} async-done(((bf16[64,4096]{1,0:T(8,128)(2,1)}), bf16[128,4096]{1,0:T(8,128)(2,1)}) %all-gather.8.cloned.1.call-update) | async-done | bytes 1048592 | tf_op jit(solution)/shard_map/all_gather | solution.py:27
  131.0 2.3 copy.28
  133.3 7.1 %all-to-all-start = ((bf16[128,32,128]{0,2,1:T(8,128)(2,1)}), bf16[128,32,128]{0,2,1:T(8,128)(2,1)S(1)}, u32[]{:S(2)}, u32[]{:S(2)}) async-start(bf16[128,32,128]{0,2,1:T(8,128)(2,1)} %bitcast.6), calls=%async_computation | async-start | bytes 2097152 | tf_op jit(solution)/shard_map/all_to_all | solution.py:33
  140.4 0.7 convert_multiply_fusion.5
  141.1 92.0 %all-to-all-done = bf16[128,32,128]{0,2,1:T(8,128)(2,1)S(1)} async-done(((bf16[128,32,128]{0,2,1:T(8,128)(2,1)}), bf16[128,32,128]{0,2,1:T(8,128)(2,1)S(1)}, u32[]{:S(2)}, u32[]{:S(2)}) %all-to-all-start) | async-done | bytes 1048608 | tf_op jit(solution)/shard_map/all_to_all | solution.py:33
  233.1 0.7 copy.29
  233.8 231.0 %all-gather.6.cloned.1.call-done = bf16[2,896,4096]{2,1,0:T(8,128)(2,1)} async-done(((bf16[2,896,512]{2,1,0:T(8,128)(2,1)}), bf16[2,896,4096]{2,1,0:T(8,128)(2,1)}) %all-gather.6.cloned.1.call-update) | async-done | bytes 14680080 | tf_op jit(solution)/shard_map/all_gather | solution.py:36
  464.9 5.4 %multiply_convert_fusion = (bf16[128,896]{0,1:T(8,128)(2,1)S(1)}, bf16[128,896]{0,1:T(8,128)(2,1)S(1)}) fusion(bf16[128,896]{0,1:T(8,128)(2,1)S(1)} %copy.26, bf16[128,896]{0,1:T(8,128)(2,1)S(1)} %copy.27, bf16[128,4096]{1,0:T(8,128)(2,1)} %all-gather.8.cloned.1.call-done, bf16[2,896,4096]{2,1,0:T(8,128)(2,1)} %all-gather.6.cloned.1.call-done), kind=kOutput, calls=%fused_computation.27 | convolution fusion | flops 941359104 | bytes 9306112 | tf_op jit(solution)/shard_map/dot_general | solution.py:37
  470.3 0.8 copy.31
  471.2 0.8 copy.30
  472.0 6.4 %fusion.10 = (bf16[896,128]{1,0:T(8,128)(2,1)}, f32[896,128]{1,0:T(8,128)}, f32[896,128]{1,0:T(8,128)}) fusion(bf16[896,128]{1,0:T(8,128)(2,1)S(1)} %copy-done, f32[896]{0:T(1024)S(1)} %convert_multiply_fusion.5, f32[896,128]{1,0:T(8,128)S(1)} %copy-done.1, f32[896,128]{1,0:T(8,128)S(1)} %copy-done.2, bf16[4096,128]{1,0:T(8,128)(2,1)S(1)} %bitcast.27, ...), kind=kOutput, calls=%fused_computation.19 | convolution fusion | flops 941588480 | bytes 10685952 | tf_op jit(solution)/shard_map/dot_general | solution.py:43
  (6 shorter events, 0.0 us)
Async XLA Ops:
  7.2 46.8 %all-gather.4.cloned.1.call-start = ((), (), s32[]{:S(2)}) async-start(), calls=%async_computation.1 | async-start | bytes 2293760 | tf_op jit(solution)/shard_map/all_gather | solution.py:35
  9.6 462.4 %copy-start = (bf16[896,128]{1,0:T(8,128)(2,1)S(1)}, bf16[896,128]{1,0:T(8,128)(2,1)}, u32[]{:S(2)}) copy-start(bf16[896,128]{1,0:T(8,128)(2,1)} %param.10) | copy-start | bytes 688132
  9.6 462.4 %copy-start.1 = (f32[896,128]{1,0:T(8,128)S(1)}, f32[896,128]{1,0:T(8,128)}, u32[]{:S(2)}) copy-start(f32[896,128]{1,0:T(8,128)} %param.11) | copy-start | bytes 1376260
  11.4 119.5 %all-gather.8.cloned.1.call-start = ((), (), s32[]{:S(2)}) async-start(), calls=%async_computation.3 | async-start | bytes 1572864 | tf_op jit(solution)/shard_map/all_gather | solution.py:27
  24.8 440.1 %all-gather.6.cloned.1.call-start = ((), (), s32[]{:S(2)}) async-start(), calls=%async_computation.2 | async-start | bytes 16515072 | tf_op jit(solution)/shard_map/all_gather | solution.py:36
  133.3 99.9 %all-to-all-start = ((bf16[128,32,128]{0,2,1:T(8,128)(2,1)}), bf16[128,32,128]{0,2,1:T(8,128)(2,1)S(1)}, u32[]{:S(2)}, u32[]{:S(2)}) async-start(bf16[128,32,128]{0,2,1:T(8,128)(2,1)} %bitcast.6), calls=%async_computation | async-start | bytes 2097152 | tf_op jit(solution)/shard_map/all_to_all | solution.py:33
  233.8 238.2 %copy-start.2 = (f32[896,128]{1,0:T(8,128)S(1)}, f32[896,128]{1,0:T(8,128)}, u32[]{:S(2)}) copy-start(f32[896,128]{1,0:T(8,128)} %param.12) | copy-start | bytes 1376260
Sparse Core Ops, SparseCore 0:
  11.6 42.3 all-gather.3
  56.1 74.8 all-gather.7
  133.1 331.7 all-gather.5
